TPU v7x, 32 devices: a whole 2x2x4 slice. The times are simulated.
32 devices in a mesh: grp: 4 (over y, core), row: 8 (over z, x).
Axes of the slice: x: 2, y: 2, z: 4, core: 2. Of those that a mesh axis runs over, the one named last changes fastest.
Arguments:
- labeled: bfloat16 [4, 1024, 1024], P(None, 'row', 'grp'), may hold values from -6 to 6
- candidates: bfloat16 [4096, 1024], P(('grp', 'row')), may hold values from -6 to 6
- factor_rows: bfloat16 [4, 1024, 4096], P(None, 'row'), may hold values from -6 to 6
- block_inverse: bfloat16 [4, 1024, 1024], P(None, 'row'), as said below
Outputs:
- whitened: bfloat16 [4, 1024, 4096], P(None, 'row', 'grp')
- explained: float32 [4096], P('grp')
Inputs may be any that keep to these rules, and one draw needn't show every extreme that they name: Each block of block_inverse is lower triangular with a positive diagonal; it is given as is and is not derived from factor_rows.
All inputs are finite; a program needn't handle non-finite values.
Results may differ from a plain program's by a relative error of at most 0.0075.
Values may be sent and summed in bfloat16 or wider, within the bound.
No kernel may reach another device: no remote copies, remote signals or barrier semaphores. Data moves between devices by JAX's collectives and lax.ppermute only.
A program may use at most 64 MiB of HBM per device.

v0:
```python
import math
import jax
import jax.numpy as jnp
from jax import lax
from jax.sharding import PartitionSpec as P


def on_device(labeled, candidates, factor_rows, block_inverse):
    gathered = lax.all_gather(labeled, "grp", axis=2, tiled=True)
    block_count = gathered.shape[0]
    own_count = gathered.shape[1]
    feature_width = gathered.shape[2]
    block_size = block_inverse.shape[2]
    kernel_scale = 0.5 / math.sqrt(feature_width)
    flat_rows = gathered.reshape(block_count * own_count, feature_width)
    kernel = jnp.exp(
        jnp.dot(
            flat_rows,
            lax.all_gather(candidates, "row", axis=0, tiled=True).T,
            preferred_element_type=jnp.float32,
        )
        * kernel_scale
    )
    cand_count = kernel.shape[1]
    kernel = kernel.reshape(block_count, own_count, cand_count)
    pending = [kernel[number] for number in range(block_count)]
    solved_own = []
    for number in range(block_count):
        rounded = pending[number].astype(jnp.bfloat16)
        residual_block = lax.all_gather(rounded, "row", axis=0, tiled=True)
        own_rows = jnp.dot(
            block_inverse[number], residual_block, preferred_element_type=jnp.float32
        ).astype(jnp.bfloat16)
        solved = lax.all_gather(own_rows, "row", axis=0, tiled=True)
        solved_own.append(own_rows)
        lower_edge = number * block_size
        upper_edge = (number + 1) * block_size
        if number + 1 < block_count:
            panel = factor_rows[number + 1 :, :, lower_edge:upper_edge]
            later_count = block_count - number - 1
            updates = jnp.dot(
                panel.reshape(later_count * own_count, block_size),
                solved,
                preferred_element_type=jnp.float32,
            )
            updates = updates.reshape(later_count, own_count, cand_count)
            for later in range(later_count):
                pending[number + 1 + later] = pending[number + 1 + later] - updates[later]
    whitened = jnp.stack(solved_own, axis=0)
    squares = jnp.sum(jnp.square(whitened.astype(jnp.float32)), axis=(0, 1))
    explained = lax.psum(squares, "row")
    return (whitened, explained)


def solution(mesh):
    in_specs = (
        P(None, "row", "grp"),
        P(("grp", "row"), None),
        P(None, "row", None),
        P(None, "row", None),
    )
    out_specs = (P(None, "row", "grp"), P("grp"))
    return jax.shard_map(
        on_device, mesh=mesh, in_specs=in_specs, out_specs=out_specs, check_vma=False
    )
```

profile of v0, /device:TPU:0, one launch (start us, length us, event | category | flops | bytes accessed | tf_op | source)
XLA Modules:
  0.0 468.7 jit_solution(2871599879833106389)
XLA Ops:
  8.7 20.4 %all-gather.10.cloned.1.call-done = bf16[4,128,1024]{2,1,0:T(8,128)(2,1)} async-done(((bf16[4,128,256]{2,1,0:T(8,128)(2,1)}), bf16[4,128,1024]{2,1,0:T(8,128)(2,1)}) %all-gather.10.cloned.1.call-update) | async-done | bytes 1048592 | tf_op jit(solution)/shard_map/all_gather | solution.py:9
  29.1 51.2 %all-gather.12.cloned.1.call-done = bf16[1024,1024]{1,0:T(8,128)(2,1)} async-done(((bf16[128,1024]{1,0:T(8,128)(2,1)}), bf16[1024,1024]{1,0:T(8,128)(2,1)}) %all-gather.12.cloned.1.call-update) | async-done | bytes 2097168 | tf_op jit(solution)/shard_map/all_gather | solution.py:19
  80.3 3.3 multiply_exponential_fusion
  83.7 0.8 slice.122
  84.5 47.7 %all-gather.14.cloned.1.call-done = bf16[1024,1024]{1,0:T(8,128)(2,1)} async-done(((bf16[128,1024]{1,0:T(8,128)(2,1)}), bf16[1024,1024]{1,0:T(8,128)(2,1)}) %all-gather.14.cloned.1.call-update) | async-done | bytes 2097168 | tf_op jit(solution)/shard_map/all_gather | solution.py:30
  132.3 2.7 convolution_convert_fusion.3
  135.1 2.1 slice.61
  137.1 45.7 %all-gather.16.cloned.1.call-done = bf16[1024,1024]{1,0:T(8,128)(2,1)} async-done(((bf16[128,1024]{1,0:T(8,128)(2,1)}), bf16[1024,1024]{1,0:T(8,128)(2,1)}) %all-gather.16.cloned.1.call-update) | async-done | bytes 2097168 | tf_op jit(solution)/shard_map/all_gather | solution.py:34
  182.8 2.8 convolution_bitcast_fusion
  185.6 1.2 copy-done.4
  187.6 47.7 %all-gather.18.cloned.1.call-done = bf16[1024,1024]{1,0:T(8,128)(2,1)} async-done(((bf16[128,1024]{1,0:T(8,128)(2,1)}), bf16[1024,1024]{1,0:T(8,128)(2,1)}) %all-gather.18.cloned.1.call-update) | async-done | bytes 2097168 | tf_op jit(solution)/shard_map/all_gather | solution.py:30
  235.4 2.7 convolution_convert_fusion.2
  238.2 1.1 slice.66
  239.3 46.6 %all-gather.20.cloned.1.call-done = bf16[1024,1024]{1,0:T(8,128)(2,1)} async-done(((bf16[128,1024]{1,0:T(8,128)(2,1)}), bf16[1024,1024]{1,0:T(8,128)(2,1)}) %all-gather.20.cloned.1.call-update) | async-done | bytes 2097168 | tf_op jit(solution)/shard_map/all_gather | solution.py:34
  285.9 2.3 convolution_bitcast_fusion.1
  288.2 1.8 fusion.3
  290.1 47.7 %all-gather.22.cloned.1.call-done = bf16[1024,1024]{1,0:T(8,128)(2,1)} async-done(((bf16[128,1024]{1,0:T(8,128)(2,1)}), bf16[1024,1024]{1,0:T(8,128)(2,1)}) %all-gather.22.cloned.1.call-update) | async-done | bytes 2097168 | tf_op jit(solution)/shard_map/all_gather | solution.py:30
  337.8 2.8 convolution_convert_fusion.1
  340.8 47.7 %all-gather.24.cloned.1.call-done = bf16[1024,1024]{1,0:T(8,128)(2,1)} async-done(((bf16[128,1024]{1,0:T(8,128)(2,1)}), bf16[1024,1024]{1,0:T(8,128)(2,1)}) %all-gather.24.cloned.1.call-update) | async-done | bytes 2097168 | tf_op jit(solution)/shard_map/all_gather | solution.py:34
  388.5 2.9 fusion.1
  391.4 47.8 %all-gather.26.cloned.1.call-done = bf16[1024,1024]{1,0:T(8,128)(2,1)} async-done(((bf16[128,1024]{1,0:T(8,128)(2,1)}), bf16[1024,1024]{1,0:T(8,128)(2,1)}) %all-gather.26.cloned.1.call-update) | async-done | bytes 2097168 | tf_op jit(solution)/shard_map/all_gather | solution.py:30
  439.2 2.1 fusion.2
  441.4 1.3 multiply_reduce_fusion
  442.6 19.5 %psum.7 = f32[1024]{0:T(1024)} all-reduce(f32[1024]{0:T(1024)S(1)} %get-tuple-element.2), channel_id=1, replica_groups=mesh['grp'=4,'row'=8] {'row'}, use_global_device_ids=true, to_apply=%region_1.0 | all-reduce | flops 1024 | bytes 8192 | tf_op jit(solution)/shard_map/psum | solution.py:51
  (32 shorter events, 2.6 us)
Async XLA Ops:
  7.2 21.9 %all-gather.10.cloned.1.call-start = ((), (), s32[]{:S(2)}) async-start(), calls=%async_computation | async-start | bytes 1310720 | tf_op jit(solution)/shard_map/all_gather | solution.py:9
  7.9 72.4 %all-gather.12.cloned.1.call-start = ((), (), s32[]{:S(2)}) async-start(), calls=%async_computation.1 | async-start | bytes 2359296 | tf_op jit(solution)/shard_map/all_gather | solution.py:19
  8.6 123.6 %all-gather.14.cloned.1.call-start = ((), (), s32[]{:S(2)}) async-start(), calls=%async_computation.2 | async-start | bytes 2359296 | tf_op jit(solution)/shard_map/all_gather | solution.py:30
  80.3 51.9 %copy-start.6 = (bf16[4,128,1024]{2,1,0:T(8,128)(2,1)S(1)}, bf16[4,128,1024]{2,1,0:T(8,128)(2,1)}, u32[]{:S(2)}) copy-start(bf16[4,128,1024]{2,1,0:T(8,128)(2,1)} %param.7) | copy-start | bytes 3145732
  83.7 102.0 %copy-start.3 = (f32[512,1024]{1,0:T(8,128)}, f32[512,1024]{1,0:T(8,128)S(1)}, u32[]{:S(2)}) copy-start(f32[512,1024]{1,0:T(8,128)S(1)} %multiply_exponential_fusion) | copy-start | bytes 6291460
  84.5 98.3 %all-gather.16.cloned.1.call-start = ((), (), s32[]{:S(2)}) async-start(), calls=%async_computation.3 | async-start | bytes 2359296 | tf_op jit(solution)/shard_map/all_gather | solution.py:34
  135.0 100.3 %all-gather.18.cloned.1.call-start = ((), (), s32[]{:S(2)}) async-start(), calls=%async_computation.4 | async-start | bytes 2359296 | tf_op jit(solution)/shard_map/all_gather | solution.py:30
  185.6 1.2 copy-start.4
  187.6 98.3 %all-gather.20.cloned.1.call-start = ((), (), s32[]{:S(2)}) async-start(), calls=%async_computation.5 | async-start | bytes 2359296 | tf_op jit(solution)/shard_map/all_gather | solution.py:34
  238.1 99.7 %all-gather.22.cloned.1.call-start = ((), (), s32[]{:S(2)}) async-start(), calls=%async_computation.6 | async-start | bytes 2359296 | tf_op jit(solution)/shard_map/all_gather | solution.py:30
  239.3 48.9 %copy-start.5 = (f32[384,1024]{1,0:T(8,128)S(1)}, f32[384,1024]{1,0:T(8,128)}, u32[]{:S(2)}) copy-start(f32[384,1024]{1,0:T(8,128)} %copy-done.4) | copy-start | bytes 4718596
  290.1 98.4 %all-gather.24.cloned.1.call-start = ((), (), s32[]{:S(2)}) async-start(), calls=%async_computation.7 | async-start | bytes 2359296 | tf_op jit(solution)/shard_map/all_gather | solution.py:34
  340.7 98.5 %all-gather.26.cloned.1.call-start = ((), (), s32[]{:S(2)}) async-start(), calls=%async_computation.8 | async-start | bytes 2359296 | tf_op jit(solution)/shard_map/all_gather | solution.py:30
  391.4 49.9 %copy-start = (bf16[1024,128]{0,1:T(8,128)(2,1)S(1)}, bf16[1024,128]{0,1:T(8,128)(2,1)}, u32[]{:S(2)}) copy-start(bf16[1024,128]{0,1:T(8,128)(2,1)} %convolution_convert_fusion.3) | copy-start | bytes 786436
  391.4 50.0 %copy-start.1 = (bf16[1024,128]{0,1:T(8,128)(2,1)S(1)}, bf16[1024,128]{0,1:T(8,128)(2,1)}, u32[]{:S(2)}) copy-start(bf16[1024,128]{0,1:T(8,128)(2,1)} %convolution_convert_fusion.2) | copy-start | bytes 786436
  391.4 50.0 %copy-start.2 = (bf16[1024,128]{0,1:T(8,128)(2,1)S(1)}, bf16[1024,128]{0,1:T(8,128)(2,1)}, u32[]{:S(2)}) copy-start(bf16[1024,128]{0,1:T(8,128)(2,1)} %convolution_convert_fusion.1) | copy-start | bytes 786436
Sparse Core Ops, SparseCore 0:
  9.5 19.5 all-gather.9
  31.2 49.0 all-gather.11
  84.6 47.6 all-gather.13
  135.1 47.6 all-gather.15
  187.7 47.6 all-gather.17
  238.2 47.6 all-gather.19
  290.2 47.6 all-gather.21
  340.8 47.6 all-gather.23
  391.6 47.6 all-gather.25
where the time goes:
time: 469 us
  waiting for transfers between devices  404 us (86%)
  matrix products  21.8 us (5%)
  blocking collectives  19.5 us (4%)
  between operations  13.9 us (3%)
  local copies, waits for them, and re-layouts  5.13 us (1%)
    all_gather x4, waiting for transfers between devices, on_device(): residual_block = lax.all_gather(rounded, 'row', axis=0, tiled=True)  191 us
    all_gather x3, waiting for transfers between devices, on_device(): solved = lax.all_gather(own_rows, 'row', axis=0, tiled=True)  140 us
    all_gather x1, waiting for transfers between devices, on_device(): lax.all_gather(candidates, 'row', axis=0, tiled=True)  51.2 us
    all_gather x1, waiting for transfers between devices, on_device(): gathered = lax.all_gather(labeled, 'grp', axis=2, tiled=True)  20.4 us
    psum x1, blocking collectives, on_device(): explained = lax.psum(squares, 'row')  19.5 us
    dot_general x4, matrix products, on_device(): jnp.dot(block_inverse[number], residual_block, preferred_element_type=jnp...  10.4 us
  transfers between devices with their start and end apart: 9, of which 9 were waited for; matrix products, arithmetic and copies ran while one was open for 1% of the time, Pallas kernels for 0%

commit v1 on v0

--- a/solution.py
+++ b/solution.py
@@ -3,6 +3,18 @@
 import jax.numpy as jnp
 from jax import lax
 from jax.sharding import PartitionSpec as P
+
+
+def gather_by_bits(value, axis, dim):
+    ways, here = (lax.axis_size(axis), lax.axis_index(axis))
+    grown, reach = (value, 1)
+    while reach < ways:
+        theirs = lax.ppermute(grown, axis, [(d, d ^ reach) for d in range(ways)])
+        mine_first = jnp.concatenate([grown, theirs], axis=dim)
+        theirs_first = jnp.concatenate([theirs, grown], axis=dim)
+        grown = jnp.where(here & reach == 0, mine_first, theirs_first)
+        reach = 2 * reach
+    return grown
 
 
 def on_device(labeled, candidates, factor_rows, block_inverse):
@@ -31,7 +43,7 @@
         own_rows = jnp.dot(
             block_inverse[number], residual_block, preferred_element_type=jnp.float32
         ).astype(jnp.bfloat16)
-        solved = lax.all_gather(own_rows, "row", axis=0, tiled=True)
+        solved = gather_by_bits(own_rows, "row", 0)
         solved_own.append(own_rows)
         lower_edge = number * block_size
         upper_edge = (number + 1) * block_size

time: 469 us -> 525 us (1.12)
  waiting for transfers between devices: 404 us -> 443 us
  starting transfers between devices: 0.37 us -> 17.2 us
    ppermute x0 -> x9, waiting for transfers between devices: none -> 175 us  [gather_by_bits(): theirs = lax.ppermute(grown, axis, [(d, d ^ reach) for d in range(ways)])]
    all_gather x3 -> x0, waiting for transfers between devices: 140 us -> none  [on_device(): solved = lax.all_gather(own_rows, 'row', axis=0, tiled=True)]
    ppermute x0 -> x9, starting transfers between devices: none -> 16.9 us  [gather_by_bits(): theirs = lax.ppermute(grown, axis, [(d, d ^ reach) for d in range(ways)])]
  transfers between devices with their start and end apart: 9 -> 15, of which waited for: 9 -> 15; matrix products, arithmetic and copies ran while one was open for 1% -> 0% of each run, Pallas kernels for 0% -> 0%
where the time goes in v1:
time: 525 us; the launch traced here: 524 us
  waiting for transfers between devices  443 us (84%)
  blocking collectives  19.5 us (4%)
  matrix products  17.6 us (3%)
  starting transfers between devices  17.2 us (3%)
  between operations  14.3 us (3%)
  other arithmetic  6.75 us (1%)
  local copies, waits for them, and re-layouts  6.48 us (1%)
    all_gather x4, waiting for transfers between devices, on_device(): residual_block = lax.all_gather(rounded, 'row', axis=0, tiled=True)  195 us
    ppermute x9, waiting for transfers between devices, gather_by_bits(): theirs = lax.ppermute(grown, axis, [(d, d ^ reach) for d in range(ways)])  175 us
    all_gather x1, waiting for transfers between devices, on_device(): lax.all_gather(candidates, 'row', axis=0, tiled=True)  51.2 us
    all_gather x1, waiting for transfers between devices, on_device(): gathered = lax.all_gather(labeled, 'grp', axis=2, tiled=True)  20.4 us
    psum x1, blocking collectives, on_device(): explained = lax.psum(squares, 'row')  19.5 us
    ppermute x9, starting transfers between devices, gather_by_bits(): theirs = lax.ppermute(grown, axis, [(d, d ^ reach) for d in range(ways)])  16.9 us
  transfers between devices with their start and end apart: 15, of which 15 were waited for; matrix products, arithmetic and copies ran while one was open for 0% of the time, Pallas kernels for 0%

profile of v1, /device:TPU:0, one launch (start us, length us, event | category | flops | bytes accessed | tf_op | source)
XLA Modules:
  0.0 524.4 jit_solution(2352394604683688092)
XLA Ops:
  8.7 20.4 %all-gather.7.cloned.1.call-done = bf16[4,128,1024]{2,1,0:T(8,128)(2,1)} async-done(((bf16[4,128,256]{2,1,0:T(8,128)(2,1)}), bf16[4,128,1024]{2,1,0:T(8,128)(2,1)}) %all-gather.7.cloned.1.call-update) | async-done | bytes 1048592 | tf_op jit(solution)/shard_map/all_gather | solution.py:21
  29.1 51.2 %all-gather.9.cloned.1.call-done = bf16[1024,1024]{1,0:T(8,128)(2,1)} async-done(((bf16[128,1024]{1,0:T(8,128)(2,1)}), bf16[1024,1024]{1,0:T(8,128)(2,1)}) %all-gather.9.cloned.1.call-update) | async-done | bytes 2097168 | tf_op jit(solution)/shard_map/all_gather | solution.py:31
  80.3 3.3 multiply_exponential_fusion
  85.8 47.7 %all-gather.11.cloned.1.call-done = bf16[1024,1024]{1,0:T(8,128)(2,1)} async-done(((bf16[128,1024]{1,0:T(8,128)(2,1)}), bf16[1024,1024]{1,0:T(8,128)(2,1)}) %all-gather.11.cloned.1.call-update) | async-done | bytes 2097168 | tf_op jit(solution)/shard_map/all_gather | solution.py:42
  136.2 5.8 %collective-permute-done = bf16[128,1024]{1,0:T(8,128)(2,1)S(1)} collective-permute-done((bf16[128,1024]{1,0:T(8,128)(2,1)S(1)}, bf16[128,1024]{1,0:T(8,128)(2,1)S(1)}, u32[]{:S(2)}, u32[]{:S(2)}) %collective-permute-start) | collective-permute-done | bytes 262176 | tf_op jit(solution)/shard_map/ppermute | solution.py:12
  142.2 2.2 collective-permute-start.1
  144.3 10.0 %collective-permute-done.1 = bf16[256,1024]{1,0:T(8,128)(2,1)S(1)} collective-permute-done((bf16[256,1024]{1,0:T(8,128)(2,1)S(1)}, bf16[256,1024]{1,0:T(8,128)(2,1)S(1)}, u32[]{:S(2)}, u32[]{:S(2)}) %collective-permute-start.1) | collective-permute-done | bytes 524320 | tf_op jit(solution)/shard_map/ppermute | solution.py:12
  154.8 2.8 collective-permute-start.2
  158.8 42.1 %collective-permute-done.2 = bf16[512,1024]{1,0:T(8,128)(2,1)} collective-permute-done((bf16[512,1024]{1,0:T(8,128)(2,1)S(1)}, bf16[512,1024]{1,0:T(8,128)(2,1)}, u32[]{:S(2)}, u32[]{:S(2)}) %collective-permute-start.2) | collective-permute-done | bytes 1048608 | tf_op jit(solution)/shard_map/ppermute | solution.py:12
  201.0 2.6 fusion.21
  206.6 49.0 %all-gather.13.cloned.1.call-done = bf16[1024,1024]{1,0:T(8,128)(2,1)} async-done(((bf16[128,1024]{1,0:T(8,128)(2,1)}), bf16[1024,1024]{1,0:T(8,128)(2,1)}) %all-gather.13.cloned.1.call-update) | async-done | bytes 2097168 | tf_op jit(solution)/shard_map/all_gather | solution.py:42
  258.2 5.8 %collective-permute-done.3 = bf16[128,1024]{1,0:T(8,128)(2,1)S(1)} collective-permute-done((bf16[128,1024]{1,0:T(8,128)(2,1)S(1)}, bf16[128,1024]{1,0:T(8,128)(2,1)S(1)}, u32[]{:S(2)}, u32[]{:S(2)}) %collective-permute-start.3) | collective-permute-done | bytes 262176 | tf_op jit(solution)/shard_map/ppermute | solution.py:12
  266.4 10.0 %collective-permute-done.4 = bf16[256,1024]{1,0:T(8,128)(2,1)S(1)} collective-permute-done((bf16[256,1024]{1,0:T(8,128)(2,1)S(1)}, bf16[256,1024]{1,0:T(8,128)(2,1)S(1)}, u32[]{:S(2)}, u32[]{:S(2)}) %collective-permute-start.4) | collective-permute-done | bytes 524320 | tf_op jit(solution)/shard_map/ppermute | solution.py:12
  276.9 2.8 collective-permute-start.5
  280.8 42.1 %collective-permute-done.5 = bf16[512,1024]{1,0:T(8,128)(2,1)S(1)} collective-permute-done((bf16[512,1024]{1,0:T(8,128)(2,1)S(1)}, bf16[512,1024]{1,0:T(8,128)(2,1)S(1)}, u32[]{:S(2)}, u32[]{:S(2)}) %collective-permute-start.5) | collective-permute-done | bytes 1048608 | tf_op jit(solution)/shard_map/ppermute | solution.py:12
  326.8 49.0 %all-gather.15.cloned.1.call-done = bf16[1024,1024]{1,0:T(8,128)(2,1)} async-done(((bf16[128,1024]{1,0:T(8,128)(2,1)}), bf16[1024,1024]{1,0:T(8,128)(2,1)}) %all-gather.15.cloned.1.call-update) | async-done | bytes 2097168 | tf_op jit(solution)/shard_map/all_gather | solution.py:42
  378.4 5.8 %collective-permute-done.6 = bf16[128,1024]{1,0:T(8,128)(2,1)S(1)} collective-permute-done((bf16[128,1024]{1,0:T(8,128)(2,1)S(1)}, bf16[128,1024]{1,0:T(8,128)(2,1)S(1)}, u32[]{:S(2)}, u32[]{:S(2)}) %collective-permute-start.6) | collective-permute-done | bytes 262176 | tf_op jit(solution)/shard_map/ppermute | solution.py:12
  384.4 2.2 collective-permute-start.7
  386.6 10.0 %collective-permute-done.7 = bf16[256,1024]{1,0:T(8,128)(2,1)S(1)} collective-permute-done((bf16[256,1024]{1,0:T(8,128)(2,1)S(1)}, bf16[256,1024]{1,0:T(8,128)(2,1)S(1)}, u32[]{:S(2)}, u32[]{:S(2)}) %collective-permute-start.7) | collective-permute-done | bytes 524320 | tf_op jit(solution)/shard_map/ppermute | solution.py:12
  397.1 2.8 collective-permute-start.8
  399.9 43.2 %collective-permute-done.8 = bf16[512,1024]{1,0:T(8,128)(2,1)S(1)} collective-permute-done((bf16[512,1024]{1,0:T(8,128)(2,1)S(1)}, bf16[512,1024]{1,0:T(8,128)(2,1)S(1)}, u32[]{:S(2)}, u32[]{:S(2)}) %collective-permute-start.8) | collective-permute-done | bytes 1048608 | tf_op jit(solution)/shard_map/ppermute | solution.py:12
  443.1 2.6 fusion.26
  445.7 49.0 %all-gather.17.cloned.1.call-done = bf16[1024,1024]{1,0:T(8,128)(2,1)} async-done(((bf16[128,1024]{1,0:T(8,128)(2,1)}), bf16[1024,1024]{1,0:T(8,128)(2,1)}) %all-gather.17.cloned.1.call-update) | async-done | bytes 2097168 | tf_op jit(solution)/shard_map/all_gather | solution.py:42
  498.0 19.5 %psum.7 = f32[1024]{0:T(1024)} all-reduce(f32[1024]{0:T(1024)S(1)} %get-tuple-element.2), channel_id=1, replica_groups=mesh['grp'=4,'row'=8] {'row'}, use_global_device_ids=true, to_apply=%region_1.2 | all-reduce | flops 1024 | bytes 8192 | tf_op jit(solution)/shard_map/psum | solution.py:63
  (45 shorter events, 28.1 us)
Async XLA Ops:
  7.2 21.9 %all-gather.7.cloned.1.call-start = ((), (), s32[]{:S(2)}) async-start(), calls=%async_computation | async-start | bytes 1310720 | tf_op jit(solution)/shard_map/all_gather | solution.py:21
  7.9 72.4 %all-gather.9.cloned.1.call-start = ((), (), s32[]{:S(2)}) async-start(), calls=%async_computation.1 | async-start | bytes 2359296 | tf_op jit(solution)/shard_map/all_gather | solution.py:31
  8.6 124.9 %all-gather.11.cloned.1.call-start = ((), (), s32[]{:S(2)}) async-start(), calls=%async_computation.2 | async-start | bytes 2359296 | tf_op jit(solution)/shard_map/all_gather | solution.py:42
  80.3 53.2 %copy-start = (bf16[4,128,1024]{2,1,0:T(8,128)(2,1)S(1)}, bf16[4,128,1024]{2,1,0:T(8,128)(2,1)}, u32[]{:S(2)}) copy-start(bf16[4,128,1024]{2,1,0:T(8,128)(2,1)} %param.7) | copy-start | bytes 3145732
  83.7 1.3 copy-start.1
  85.8 169.8 %all-gather.13.cloned.1.call-start = ((), (), s32[]{:S(2)}) async-start(), calls=%async_computation.3 | async-start | bytes 2359296 | tf_op jit(solution)/shard_map/all_gather | solution.py:42
  135.6 6.4 %collective-permute-start = (bf16[128,1024]{1,0:T(8,128)(2,1)S(1)}, bf16[128,1024]{1,0:T(8,128)(2,1)S(1)}, u32[]{:S(2)}, u32[]{:S(2)}) collective-permute-start(bf16[128,1024]{1,0:T(8,128)(2,1)S(1)} %bitcast.49), channel_id=1, source_target_pairs={{0,1},{1,0},{2,3},{3,2},{4,5},{5,4},{6,7},{7,6},{8,9},{9,8},{10,11... | collective-permute-start | bytes 786440 | tf_op jit(solution)/shard_map/ppermute | solution.py:12
  142.2 12.2 %collective-permute-start.1 = (bf16[256,1024]{1,0:T(8,128)(2,1)S(1)}, bf16[256,1024]{1,0:T(8,128)(2,1)S(1)}, u32[]{:S(2)}, u32[]{:S(2)}) collective-permute-start(bf16[256,1024]{1,0:T(8,128)(2,1)S(1)} %maximum_select_fusion.15), channel_id=1, source_target_pairs={{0,2},{1,3},{2,0},{3,1},{4,6},{5,7},{6,4},{7,5},{8,10},{9,11},{10,... | collective-permute-start | bytes 1572872 | tf_op jit(solution)/shard_map/ppermute | solution.py:12
  154.8 46.1 %collective-permute-start.2 = (bf16[512,1024]{1,0:T(8,128)(2,1)S(1)}, bf16[512,1024]{1,0:T(8,128)(2,1)}, u32[]{:S(2)}, u32[]{:S(2)}) collective-permute-start(bf16[512,1024]{1,0:T(8,128)(2,1)S(1)} %maximum_select_fusion.12), channel_id=1, source_target_pairs={{0,4},{1,5},{2,6},{3,7},{4,0},{5,1},{6,2},{7,3},{8,12},{9,13},{10,... | collective-permute-start | bytes 3145736 | tf_op jit(solution)/shard_map/ppermute | solution.py:12
  203.5 1.2 copy-start.2
  206.5 169.2 %all-gather.15.cloned.1.call-start = ((), (), s32[]{:S(2)}) async-start(), calls=%async_computation.4 | async-start | bytes 2359296 | tf_op jit(solution)/shard_map/all_gather | solution.py:42
  257.6 6.4 %collective-permute-start.3 = (bf16[128,1024]{1,0:T(8,128)(2,1)S(1)}, bf16[128,1024]{1,0:T(8,128)(2,1)S(1)}, u32[]{:S(2)}, u32[]{:S(2)}) collective-permute-start(bf16[128,1024]{1,0:T(8,128)(2,1)S(1)} %bitcast.52), channel_id=1, source_target_pairs={{0,1},{1,0},{2,3},{3,2},{4,5},{5,4},{6,7},{7,6},{8,9},{9,8},{10,11... | collective-permute-start | bytes 786440 | tf_op jit(solution)/shard_map/ppermute | solution.py:12
  264.2 12.2 %collective-permute-start.4 = (bf16[256,1024]{1,0:T(8,128)(2,1)S(1)}, bf16[256,1024]{1,0:T(8,128)(2,1)S(1)}, u32[]{:S(2)}, u32[]{:S(2)}) collective-permute-start(bf16[256,1024]{1,0:T(8,128)(2,1)S(1)} %maximum_select_fusion.16), channel_id=1, source_target_pairs={{0,2},{1,3},{2,0},{3,1},{4,6},{5,7},{6,4},{7,5},{8,10},{9,11},{10,... | collective-permute-start | bytes 1572872 | tf_op jit(solution)/shard_map/ppermute | solution.py:12
  276.9 46.0 %collective-permute-start.5 = (bf16[512,1024]{1,0:T(8,128)(2,1)S(1)}, bf16[512,1024]{1,0:T(8,128)(2,1)S(1)}, u32[]{:S(2)}, u32[]{:S(2)}) collective-permute-start(bf16[512,1024]{1,0:T(8,128)(2,1)S(1)} %maximum_select_fusion.13), channel_id=1, source_target_pairs={{0,4},{1,5},{2,6},{3,7},{4,0},{5,1},{6,2},{7,3},{8,12},{9,13},{10,... | collective-permute-start | bytes 3145736 | tf_op jit(solution)/shard_map/ppermute | solution.py:12
  322.9 2.0 copy-start.3
  323.9 1.0 copy-start.4
  326.7 168.0 %all-gather.17.cloned.1.call-start = ((), (), s32[]{:S(2)}) async-start(), calls=%async_computation.5 | async-start | bytes 2359296 | tf_op jit(solution)/shard_map/all_gather | solution.py:42
  377.8 65.3 %copy-start.5 = (f32[256,1024]{1,0:T(8,128)S(1)}, f32[256,1024]{1,0:T(8,128)}, u32[]{:S(2)}) copy-start(f32[256,1024]{1,0:T(8,128)} %copy-done.4) | copy-start | bytes 3145732
  377.8 6.4 %collective-permute-start.6 = (bf16[128,1024]{1,0:T(8,128)(2,1)S(1)}, bf16[128,1024]{1,0:T(8,128)(2,1)S(1)}, u32[]{:S(2)}, u32[]{:S(2)}) collective-permute-start(bf16[128,1024]{1,0:T(8,128)(2,1)S(1)} %bitcast.55), channel_id=1, source_target_pairs={{0,1},{1,0},{2,3},{3,2},{4,5},{5,4},{6,7},{7,6},{8,9},{9,8},{10,11... | collective-permute-start | bytes 786440 | tf_op jit(solution)/shard_map/ppermute | solution.py:12
  384.4 12.2 %collective-permute-start.7 = (bf16[256,1024]{1,0:T(8,128)(2,1)S(1)}, bf16[256,1024]{1,0:T(8,128)(2,1)S(1)}, u32[]{:S(2)}, u32[]{:S(2)}) collective-permute-start(bf16[256,1024]{1,0:T(8,128)(2,1)S(1)} %maximum_select_fusion.17), channel_id=1, source_target_pairs={{0,2},{1,3},{2,0},{3,1},{4,6},{5,7},{6,4},{7,5},{8,10},{9,11},{10,... | collective-permute-start | bytes 1572872 | tf_op jit(solution)/shard_map/ppermute | solution.py:12
  397.1 46.0 %collective-permute-start.8 = (bf16[512,1024]{1,0:T(8,128)(2,1)S(1)}, bf16[512,1024]{1,0:T(8,128)(2,1)S(1)}, u32[]{:S(2)}, u32[]{:S(2)}) collective-permute-start(bf16[512,1024]{1,0:T(8,128)(2,1)S(1)} %maximum_select_fusion.14), channel_id=1, source_target_pairs={{0,4},{1,5},{2,6},{3,7},{4,0},{5,1},{6,2},{7,3},{8,12},{9,13},{10,... | collective-permute-start | bytes 3145736 | tf_op jit(solution)/shard_map/ppermute | solution.py:12
Sparse Core Ops, SparseCore 0:
  9.5 19.5 all-gather.6
  31.2 49.0 all-gather.8
  85.9 47.6 all-gather.10
  206.7 48.8 all-gather.12
  326.9 48.8 all-gather.14
  445.8 48.8 all-gather.16
